TPU v7x, 256 devices: a whole 4x4x8 slice. The times are simulated.
256 devices in a mesh: expert: 32 (over z, y_lo, core), blk: 8 (over x, y_hi).
Axes of the slice: x: 4, y: 4 (y_hi: 2, y_lo: 2; y = y_hi * 2 + y_lo), z: 8, core: 2. Of those that a mesh axis runs over, the one named last changes fastest.
Arguments:
- tokens: bfloat16 [16384, 7168], P(('expert', 'blk')), may hold values from -6 to 6
- expert_ids: int32 [16384, 8], P(('expert', 'blk')), may hold values from 0 to 255, all different within a row; in each aligned block of 64 rows (0 to 63, 64 to 127, ...) at most 4 rows name the same one
- gate_weights: bfloat16 [16384, 8], P(('expert', 'blk')), may hold values from 0.099609375 to 1
- w_gate: bfloat16 [32, 7168, 2048], P('expert', None, 'blk'), may hold values from -0.0625 to 0.0625
- w_up: bfloat16 [32, 7168, 2048], P('expert', None, 'blk'), may hold values from -0.0625 to 0.0625
- w_down: bfloat16 [32, 2048, 7168], P('expert', None, 'blk'), may hold values from -0.125 to 0.125
Outputs:
- mixed_out: bfloat16 [16384, 7168], P(('expert', 'blk'))
Inputs may be any that keep to these rules, and one draw needn't show every extreme that they name: `expert_ids`: each row names 8 different experts; among the 64 rows of one device no expert is named more than 4 times, a bound that some block reaches.
All inputs are finite; a program needn't handle non-finite values.
Results may differ from a plain program's by a relative error of at most 0.0057.
Values may be sent and summed in bfloat16 or wider, within the bound.
A program may use at most 64 MiB of HBM per device.

v0:
```python
from functools import partial

import jax
import jax.numpy as jnp
from jax import lax
from jax.sharding import PartitionSpec as P

CAP = 4


def slot_tables(id_rows, gate_rows, experts, capacity):
    labels = jnp.arange(experts, dtype=jnp.int32)
    matches = id_rows[:, :, None] == labels[None, None, :]
    chosen = jnp.any(matches, axis=1)
    weights = jnp.sum(jnp.where(matches, gate_rows.astype(jnp.float32)[:, :, None], 0.0), axis=1)
    counts = chosen.astype(jnp.int32)
    before = jnp.cumsum(counts, axis=0) - counts
    places = jnp.arange(capacity, dtype=jnp.int32)
    selected = chosen[:, :, None] & (before[:, :, None] == places[None, None, :])
    selector = selected.astype(jnp.bfloat16)
    weighting = jnp.where(selected, weights[:, :, None], 0.0).astype(jnp.bfloat16)
    return (selector, weighting)


def hidden_units(row_block, gate_mat, up_mat):
    gate_part = jnp.dot(row_block, gate_mat, preferred_element_type=jnp.float32)
    up_part = jnp.dot(row_block, up_mat, preferred_element_type=jnp.float32)
    return (jax.nn.silu(gate_part) * up_part).astype(jnp.bfloat16)


def down_slices(hidden, down_mat):
    total = jnp.dot(
        lax.all_gather(hidden, "blk", axis=1, tiled=True),
        down_mat,
        preferred_element_type=jnp.float32,
    )
    return total.astype(jnp.bfloat16)


def on_device(tokens, expert_ids, gate_weights, w_gate, w_up, w_down):
    gate_mat = w_gate[0]
    up_mat = w_up[0]
    down_mat = w_down[0]
    experts = lax.axis_size("expert")
    blocks = lax.axis_size("blk")
    tok_dev = tokens.shape[0]
    width = tokens.shape[1]
    tok_all, ids_all, gate_all = (
        lax.all_gather(tokens, "blk", axis=0, tiled=True),
        lax.all_gather(expert_ids, "blk", axis=0, tiled=True),
        lax.all_gather(gate_weights, "blk", axis=0, tiled=True),
    )
    tables = jax.vmap(partial(slot_tables, experts=experts, capacity=CAP))
    selector, weighting = tables(
        ids_all.reshape(blocks, tok_dev, -1), gate_all.reshape(blocks, tok_dev, -1)
    )
    outgoing = jnp.einsum(
        "btec,btd->ebcd",
        selector,
        tok_all.reshape(blocks, tok_dev, width),
        preferred_element_type=jnp.float32,
    ).astype(jnp.bfloat16)
    outgoing = outgoing.reshape(experts, blocks * CAP, width)
    received = lax.all_to_all(outgoing, "expert", split_axis=0, concat_axis=0, tiled=True)
    slot_count = received.shape[1]
    row_block = received.reshape(-1, received.shape[2])
    hidden = hidden_units(row_block, gate_mat, up_mat)
    slices = down_slices(hidden, down_mat).reshape(experts, slot_count, -1)
    returned = lax.all_to_all(slices, "expert", split_axis=0, concat_axis=0, tiled=True)
    returned = returned.reshape(experts, blocks, CAP, -1)
    partial_out = jnp.einsum(
        "btec,ebcd->btd", weighting, returned, preferred_element_type=jnp.float32
    ).astype(jnp.bfloat16)
    partial_out = partial_out.reshape(blocks * tok_dev, -1)
    mixed_out = lax.all_to_all(partial_out, "blk", split_axis=0, concat_axis=1, tiled=True)
    return mixed_out


def solution(mesh):
    return jax.shard_map(
        on_device,
        mesh=mesh,
        in_specs=(
            P(("expert", "blk"), None),
            P(("expert", "blk"), None),
            P(("expert", "blk"), None),
            P("expert", None, "blk"),
            P("expert", None, "blk"),
            P("expert", None, "blk"),
        ),
        out_specs=P(("expert", "blk"), None),
        check_vma=False,
    )
```

profile of v0, /device:TPU:56, one launch (start us, length us, event | category | flops | bytes accessed | tf_op | source)
XLA Modules:
  0.0 651.6 jit_solution(8814180843545732352)
XLA Ops:
  6.5 0.0 all-gather.5.cloned.1.call-start
  6.5 0.7 all-gather.5.cloned.1.call-update
  7.3 0.0 all-gather.7.cloned.1.call-start
  7.3 34.7 %all-gather = s32[8,64,8]{1,2,0:T(8,128)S(1)} all-gather(s32[1,64,8]{1,2,0:T(8,128)} %bitcast.46), channel_id=1, replica_groups=mesh['expert'=32,'blk'=8] {'blk'}, dimensions={0}, use_global_device_ids=true | all-gather | bytes 18432 | tf_op jit(solution)/shard_map/all_gather | solution.py:50
  42.0 0.2 fusion.15
  42.2 0.2 copy.26
  42.3 0.1 reduce-window_subtract_fusion
  42.4 0.1 copy.27
  42.5 72.3 %all-gather.5.cloned.1.call-done = bf16[512,7168]{1,0:T(8,128)(2,1)} async-done(((bf16[64,7168]{1,0:T(8,128)(2,1)}), bf16[512,7168]{1,0:T(8,128)(2,1)}) %all-gather.5.cloned.1.call-update) | async-done | bytes 7340048 | tf_op jit(solution)/shard_map/all_gather | solution.py:49
  114.8 7.2 %convolution_convert_fusion = bf16[8,32,4,7168]{3,1,2,0:T(8,128)(2,1)S(1)} fusion(bf16[8,64,7168,1]{2,1,3,0:T(8,128)(2,1)} %bitcast.42, s32[8,64,32]{1,2,0:T(8,128)S(1)} %copy.27, pred[8,64,32]{1,2,0:T(8,128)(4,1)S(1)} %fusion.15), kind=kOutput, calls=%fused_computation | convolution fusion | flops 946995200 | bytes 22102016 | tf_op jit(solution)/shard_map/btec,btd->ebcd/dot_general | solution.py:57
  122.0 24.1 %copy.28 = bf16[32,32,7168]{2,1,0:T(8,128)(2,1)S(1)} copy(bf16[32,32,7168]{2,0,1:T(8,128)(2,1)S(1)} %bitcast.39) | data formatting | bytes 29360128 | tf_op jit(solution)/shard_map/reshape | solution.py:63
  146.2 0.0 copy-start.1
  146.2 328.8 %all_to_all.26 = bf16[32,32,7168]{2,1,0:T(8,128)(2,1)S(1)} all-to-all(bf16[32,32,7168]{2,1,0:T(8,128)(2,1)S(1)} %copy.28), channel_id=1, replica_groups=mesh['expert'=32,'blk'=8] {'expert'}, dimensions={0} | all-to-all | bytes 29360128 | tf_op jit(solution)/shard_map/all_to_all | solution.py:64
  474.9 0.0 copy-done.1
  474.9 0.0 copy-start.2
  474.9 3.9 fusion.4
  478.9 0.0 copy-done.2
  478.9 4.8 fusion.12
  483.7 0.0 all-gather.7.cloned.1.call-update
  483.7 76.5 %all-gather.7.cloned.1.call-done = bf16[1024,2048]{1,0:T(8,128)(2,1)} async-done(((bf16[1024,256]{1,0:T(8,128)(2,1)}), bf16[1024,2048]{1,0:T(8,128)(2,1)}) %all-gather.7.cloned.1.call-update) | async-done | bytes 4194320 | tf_op jit(solution)/shard_map/all_gather | solution.py:33
  560.2 9.1 %fusion.6 = bf16[1024,896]{1,0:T(8,128)(2,1)} fusion(bf16[1024,2048]{1,0:T(8,128)(2,1)} %all-gather.7.cloned.1.call-done, bf16[1,2048,896]{2,1,0:T(8,128)(2,1)} %param.11), kind=kOutput, calls=%fused_computation.8 | convolution fusion | flops 3759013888 | bytes 9699328 | tf_op jit(solution)/shard_map/dot_general | solution.py:32
  569.2 0.0 copy-start
  569.2 8.7 %all-to-all-start.1 = ((bf16[32,32,896]{2,1,0:T(8,128)(2,1)}), bf16[32,32,896]{2,1,0:T(8,128)(2,1)S(1)}, u32[]{:S(2)}, u32[]{:S(2)}) async-start(bf16[32,32,896]{2,1,0:T(8,128)(2,1)} %bitcast.45), calls=%async_computation.1 | async-start | bytes 3670016 | tf_op jit(solution)/shard_map/all_to_all | solution.py:69
  577.9 0.0 copy-done
  577.9 29.5 %all-gather.1 = bf16[8,64,8]{1,2,0:T(8,128)(2,1)S(1)} all-gather(bf16[1,64,8]{1,2,0:T(8,128)(2,1)S(1)} %bitcast.47), channel_id=1, replica_groups=mesh['expert'=32,'blk'=8] {'blk'}, dimensions={0}, use_global_device_ids=true | all-gather | bytes 9216 | tf_op jit(solution)/shard_map/all_gather | solution.py:51
  607.4 0.2 select_reduce_fusion
  607.7 15.1 %all-to-all-done.1 = bf16[32,32,896]{2,1,0:T(8,128)(2,1)S(1)} async-done(((bf16[32,32,896]{2,1,0:T(8,128)(2,1)}), bf16[32,32,896]{2,1,0:T(8,128)(2,1)S(1)}, u32[]{:S(2)}, u32[]{:S(2)}) %all-to-all-start.1) | async-done | bytes 1835040 | tf_op jit(solution)/shard_map/all_to_all | solution.py:69
  622.8 0.6 copy.29
  623.4 0.5 bitcast_convert_fusion
  623.9 19.8 %all_to_all.27 = bf16[8,64,896]{2,1,0:T(8,128)(2,1)S(1)} all-to-all(bf16[8,64,896]{2,1,0:T(8,128)(2,1)S(1)} %bitcast_convert_fusion), channel_id=1, replica_groups=mesh['expert'=32,'blk'=8] {'blk'}, dimensions={0} | all-to-all | bytes 1835008 | tf_op jit(solution)/shard_map/all_to_all | solution.py:75
  643.7 1.1 copy.33
  (1 shorter events, 0.0 us)
Async XLA Ops:
  6.5 108.3 %all-gather.5.cloned.1.call-start = ((), (), s32[]{:S(2)}) async-start(), calls=%async_computation.3 | async-start | bytes 8257536 | tf_op jit(solution)/shard_map/all_gather | solution.py:49
  7.3 552.9 %all-gather.7.cloned.1.call-start = ((), (), s32[]{:S(2)}) async-start(), calls=%async_computation.4 | async-start | bytes 4718592 | tf_op jit(solution)/shard_map/all_gather | solution.py:33
  146.2 328.8 %copy-start.1 = (bf16[1,7168,256]{2,1,0:T(8,128)(2,1)S(1)}, bf16[1,7168,256]{2,1,0:T(8,128)(2,1)}, u32[]{:S(2)}) copy-start(bf16[1,7168,256]{2,1,0:T(8,128)(2,1)} %param.9) | copy-start | bytes 11010052
  474.9 4.0 copy-start.2
  569.2 8.7 %copy-start = (bf16[64,8]{0,1:T(8,128)(2,1)S(1)}, bf16[64,8]{0,1:T(8,128)(2,1)}, u32[]{:S(2)}) copy-start(bf16[64,8]{0,1:T(8,128)(2,1)} %param.8) | copy-start | bytes 3076
  569.2 53.6 %all-to-all-start.1 = ((bf16[32,32,896]{2,1,0:T(8,128)(2,1)}), bf16[32,32,896]{2,1,0:T(8,128)(2,1)S(1)}, u32[]{:S(2)}, u32[]{:S(2)}) async-start(bf16[32,32,896]{2,1,0:T(8,128)(2,1)} %bitcast.45), calls=%async_computation.1 | async-start | bytes 3670016 | tf_op jit(solution)/shard_map/all_to_all | solution.py:69
Sparse Core Ops, SparseCore 0:
  9.9 104.8 all-gather.4
  483.8 76.2 all-gather.6
where the time goes:
time: 653 us; the launch traced here: 652 us
  blocking collectives  413 us (63%)
  waiting for transfers between devices  165 us (25%)
  local copies, waits for them, and re-layouts  26.1 us (4%)
  matrix products  25.5 us (4%)
  between operations  13.5 us (2%)
  starting transfers between devices  8.71 us (1%)
    all_to_all x1, blocking collectives, on_device(): lax.all_to_all(outgoing, 'expert', split_axis=0, concat_axis=0, tiled=True)  329 us
    all_gather x1, waiting for transfers between devices, down_slices(): lax.all_gather(hidden, 'blk', axis=1, tiled=True)  76.5 us
    all_gather x1, waiting for transfers between devices, on_device(): lax.all_gather(tokens, 'blk', axis=0, tiled=True)  72.3 us
    all_gather x1, blocking collectives, on_device(): lax.all_gather(expert_ids, 'blk', axis=0, tiled=True)  34.7 us
    all_gather x1, blocking collectives, on_device(): lax.all_gather(gate_weights, 'blk', axis=0, tiled=True)  29.5 us
    reshape x1, local copies, waits for them, and re-layouts, on_device(): outgoing = outgoing.reshape(experts, blocks * CAP, width)  24.1 us
    all_to_all x1, blocking collectives, on_device(): lax.all_to_all(partial_out, 'blk', split_axis=0, concat_axis=1, tiled=True)  19.8 us
    all_to_all x1, waiting for transfers between devices, on_device(): lax.all_to_all(slices, 'expert', split_axis=0, concat_axis=0, tiled=True)  15.1 us
  transfers between devices with their start and end apart: 3, of which 3 were waited for; matrix products, arithmetic and copies ran while one was open for 0% of the time, Pallas kernels for 0%

commit v1 on v0

--- a/solution.py
+++ b/solution.py
@@ -1,5 +1,3 @@
-from functools import partial
-
 import jax
 import jax.numpy as jnp
 from jax import lax
@@ -28,15 +26,6 @@
     return (jax.nn.silu(gate_part) * up_part).astype(jnp.bfloat16)
 
 
-def down_slices(hidden, down_mat):
-    total = jnp.dot(
-        lax.all_gather(hidden, "blk", axis=1, tiled=True),
-        down_mat,
-        preferred_element_type=jnp.float32,
-    )
-    return total.astype(jnp.bfloat16)
-
-
 def on_device(tokens, expert_ids, gate_weights, w_gate, w_up, w_down):
     gate_mat = w_gate[0]
     up_mat = w_up[0]
@@ -45,35 +34,28 @@
     blocks = lax.axis_size("blk")
     tok_dev = tokens.shape[0]
     width = tokens.shape[1]
-    tok_all, ids_all, gate_all = (
-        lax.all_gather(tokens, "blk", axis=0, tiled=True),
-        lax.all_gather(expert_ids, "blk", axis=0, tiled=True),
-        lax.all_gather(gate_weights, "blk", axis=0, tiled=True),
-    )
-    tables = jax.vmap(partial(slot_tables, experts=experts, capacity=CAP))
-    selector, weighting = tables(
-        ids_all.reshape(blocks, tok_dev, -1), gate_all.reshape(blocks, tok_dev, -1)
-    )
+    selector, weighting = slot_tables(expert_ids, gate_weights, experts, CAP)
     outgoing = jnp.einsum(
-        "btec,btd->ebcd",
-        selector,
-        tok_all.reshape(blocks, tok_dev, width),
-        preferred_element_type=jnp.float32,
+        "tec,td->ecd", selector, tokens, preferred_element_type=jnp.float32
     ).astype(jnp.bfloat16)
-    outgoing = outgoing.reshape(experts, blocks * CAP, width)
     received = lax.all_to_all(outgoing, "expert", split_axis=0, concat_axis=0, tiled=True)
-    slot_count = received.shape[1]
-    row_block = received.reshape(-1, received.shape[2])
+    mine = received.reshape(experts * CAP, width)
+    row_block = lax.all_gather(mine, "blk", axis=0, tiled=True)
     hidden = hidden_units(row_block, gate_mat, up_mat)
-    slices = down_slices(hidden, down_mat).reshape(experts, slot_count, -1)
+    hidden_all = lax.all_gather(hidden, "blk", axis=1, tiled=True)
+    slices = jnp.dot(hidden_all, down_mat, preferred_element_type=jnp.float32).astype(jnp.bfloat16)
+    slices = slices.reshape(blocks, experts, CAP, -1).transpose(1, 0, 2, 3)
+    slices = slices.reshape(experts, blocks * CAP, -1)
+    weighting_all = lax.all_gather(
+        weighting.reshape(tok_dev, experts * CAP), "blk", axis=0, tiled=True
+    ).reshape(blocks, tok_dev, experts, CAP)
     returned = lax.all_to_all(slices, "expert", split_axis=0, concat_axis=0, tiled=True)
     returned = returned.reshape(experts, blocks, CAP, -1)
     partial_out = jnp.einsum(
-        "btec,ebcd->btd", weighting, returned, preferred_element_type=jnp.float32
+        "btec,ebcd->btd", weighting_all, returned, preferred_element_type=jnp.float32
     ).astype(jnp.bfloat16)
     partial_out = partial_out.reshape(blocks * tok_dev, -1)
-    mixed_out = lax.all_to_all(partial_out, "blk", split_axis=0, concat_axis=1, tiled=True)
-    return mixed_out
+    return lax.all_to_all(partial_out, "blk", split_axis=0, concat_axis=1, tiled=True)
 
 
 def solution(mesh):

time: 653 us -> 427 us (0.65)
  blocking collectives: 413 us -> 108 us
  waiting for transfers between devices: 165 us -> 257 us
  local copies, waits for them, and re-layouts: 26.1 us -> 13.3 us
    all_to_all x1, blocking collectives: 329 us -> 54.3 us  [on_device(): lax.all_to_all(outgoing, 'expert', split_axis=0, concat_axis=0, tiled=True)]
    all_gather x2, waiting for transfers between devices: 149 us -> 247 us  [the longest x1 167 us: on_device(): row_block = lax.all_gather(mine, 'blk', axis=0, tiled=True)]
    all_gather x2 -> x1, blocking collectives: 64.2 us -> 34.3 us  [on_device(): lax.all_gather(weighting.reshape(tok_dev, experts * CAP), 'blk', axis=0,...]
    reshape x1 -> x5, local copies, waits for them, and re-layouts: 24.1 us -> 6.86 us  [the longest x2 3.41 us: on_device(): slices = slices.reshape(blocks, experts, CAP, -1).transpose(1, 0, 2, 3)]
    dot_general x3, matrix products: 16.8 us -> 10.2 us  [the longest x1 9.07 us: on_device(): jnp.dot(hidden_all, down_mat, preferred_element_type=jnp.float32)]
where the time goes in v1:
time: 427 us; the launch traced here: 426 us
  waiting for transfers between devices  257 us (60%)
  blocking collectives  108 us (25%)
  matrix products  23.8 us (6%)
  between operations  13.6 us (3%)
  local copies, waits for them, and re-layouts  13.3 us (3%)
  starting transfers between devices  8.77 us (2%)
    all_gather x1, waiting for transfers between devices, on_device(): row_block = lax.all_gather(mine, 'blk', axis=0, tiled=True)  167 us
    all_gather x1, waiting for transfers between devices, on_device(): hidden_all = lax.all_gather(hidden, 'blk', axis=1, tiled=True)  80.3 us
    all_to_all x1, blocking collectives, on_device(): lax.all_to_all(outgoing, 'expert', split_axis=0, concat_axis=0, tiled=True)  54.3 us
    all_gather x1, blocking collectives, on_device(): lax.all_gather(weighting.reshape(tok_dev, experts * CAP), 'blk', axis=0,...  34.3 us
    all_to_all x1, blocking collectives, on_device(): lax.all_to_all(partial_out, 'blk', split_axis=0, concat_axis=1, tiled=True)  19.8 us
    all_to_all x1, waiting for transfers between devices, on_device(): lax.all_to_all(slices, 'expert', split_axis=0, concat_axis=0, tiled=True)  9.7 us
    dot_general x1, matrix products, on_device(): jnp.dot(hidden_all, down_mat, preferred_element_type=jnp.float32)  9.07 us
    dot_general x1, matrix products, hidden_units(): gate_part = jnp.dot(row_block, gate_mat, preferred_element_type=jnp.float32)  8.83 us
  transfers between devices with their start and end apart: 3, of which 3 were waited for; matrix products, arithmetic and copies ran while one was open for 0% of the time, Pallas kernels for 0%

profile of v1, /device:TPU:56, one launch (start us, length us, event | category | flops | bytes accessed | tf_op | source)
XLA Modules:
  0.0 425.7 jit_solution(4727964634798736242)
XLA Ops:
  6.5 0.0 copy-start
  6.5 0.0 all-gather.3.cloned.1.call-start
  6.5 0.8 fusion.17
  7.3 0.1 copy.44
  7.4 0.1 reduce_window_sum.11
  7.6 0.1 copy.45
  7.7 0.1 copy-done
  7.7 0.6 convolution_convert_fusion
  8.4 1.4 copy.51
  9.8 54.3 %all_to_all.26 = bf16[32,4,7168]{2,1,0:T(4,128)(2,1)S(1)} all-to-all(bf16[32,4,7168]{2,1,0:T(4,128)(2,1)S(1)} %copy.51), channel_id=1, replica_groups=mesh['expert'=32,'blk'=8] {'expert'}, dimensions={0} | all-to-all | bytes 3670016 | tf_op jit(solution)/shard_map/all_to_all | solution.py:41
  64.1 1.4 reshape.42
  65.5 0.0 all-gather.3.cloned.1.call-update
  65.6 0.2 all-gather.5.cloned.1.call-start
  65.8 166.8 %all-gather.3.cloned.1.call-done = bf16[1024,7168]{1,0:T(8,128)(2,1)} async-done(((bf16[128,7168]{1,0:T(8,128)(2,1)}), bf16[1024,7168]{1,0:T(8,128)(2,1)}) %all-gather.3.cloned.1.call-update) | async-done | bytes 14680080 | tf_op jit(solution)/shard_map/all_gather | solution.py:43
  232.6 0.0 copy-start.3
  232.6 0.0 copy-start.4
  232.6 8.8 %fusion.4 = f32[1024,256]{1,0:T(8,128)S(1)} fusion(bf16[1024,7168]{1,0:T(8,128)(2,1)} %all-gather.3.cloned.1.call-done, bf16[1,7168,256]{2,1,0:T(8,128)(2,1)} %param.9), kind=kOutput, calls=%fused_computation.5 | convolution fusion | flops 3758096384 | bytes 19398656 | tf_op jit(solution)/shard_map/dot_general | solution.py:24
  241.5 1.5 copy-done.3
  243.0 1.0 copy-done.4
  244.1 4.8 %fusion.12 = bf16[1024,256]{1,0:T(8,128)(2,1)} fusion(bf16[1024,7168]{1,0:T(8,128)(2,1)S(1)} %copy-done.3, bf16[1,7168,256]{2,1,0:T(8,128)(2,1)S(1)} %copy-done.4, f32[1024,256]{1,0:T(8,128)S(1)} %fusion.4), kind=kOutput, calls=%fused_computation.10 | convolution fusion | flops 3759669248 | bytes 19922944 | tf_op jit(solution)/shard_map/dot_general | solution.py:25
  248.8 0.0 all-gather.5.cloned.1.call-update
  248.9 80.3 %all-gather.5.cloned.1.call-done = bf16[1024,2048]{1,0:T(8,128)(2,1)} async-done(((bf16[1024,256]{1,0:T(8,128)(2,1)}), bf16[1024,2048]{1,0:T(8,128)(2,1)}) %all-gather.5.cloned.1.call-update) | async-done | bytes 4194320 | tf_op jit(solution)/shard_map/all_gather | solution.py:45
  329.2 9.1 %fusion.6 = bf16[1024,896]{1,0:T(8,128)(2,1)} fusion(bf16[1024,2048]{1,0:T(8,128)(2,1)} %all-gather.5.cloned.1.call-done, bf16[1,2048,896]{2,1,0:T(8,128)(2,1)} %param.11), kind=kOutput, calls=%fused_computation.8 | convolution fusion | flops 3759013888 | bytes 9699328 | tf_op jit(solution)/shard_map/dot_general | solution.py:46
  338.2 3.1 reshape.43
  341.4 0.3 copy.52
  341.7 0.0 copy-start.2
  341.7 0.0 copy-start.1
  341.7 1.8 copy.53
  343.5 8.5 %all-to-all-start.1 = ((bf16[32,32,896]{2,1,0:T(8,128)(2,1)}), bf16[32,32,896]{2,1,0:T(8,128)(2,1)S(1)}, u32[]{:S(2)}, u32[]{:S(2)}) async-start(bf16[32,32,896]{2,1,0:T(8,128)(2,1)} %copy.53), calls=%async_computation.1 | async-start | bytes 3670016 | tf_op jit(solution)/shard_map/all_to_all | solution.py:52
  352.1 0.1 copy.46
  352.2 0.1 copy.47
  352.3 0.0 copy-done.2
  352.3 0.0 copy-done.1
  352.4 0.1 copy.48
  352.5 0.1 eq.43
  352.6 34.3 %all_gather.9 = bf16[512,128]{1,0:T(8,128)(2,1)S(1)} all-gather(bf16[64,128]{1,0:T(8,128)(2,1)S(1)} %select_convert_fusion), channel_id=1, replica_groups=mesh['expert'=32,'blk'=8] {'blk'}, dimensions={0}, use_global_device_ids=true | all-gather | bytes 147456 | tf_op jit(solution)/shard_map/all_gather | solution.py:49
  386.9 0.1 copy.49
  387.1 0.2 reshape.41
  387.3 9.7 %all-to-all-done.1 = bf16[32,32,896]{2,1,0:T(8,128)(2,1)S(1)} async-done(((bf16[32,32,896]{2,1,0:T(8,128)(2,1)}), bf16[32,32,896]{2,1,0:T(8,128)(2,1)S(1)}, u32[]{:S(2)}, u32[]{:S(2)}) %all-to-all-start.1) | async-done | bytes 1835040 | tf_op jit(solution)/shard_map/all_to_all | solution.py:52
  397.0 0.6 copy.54
  397.5 0.5 bitcast_convert_fusion
  398.0 19.8 %all_to_all.27 = bf16[8,64,896]{2,1,0:T(8,128)(2,1)S(1)} all-to-all(bf16[8,64,896]{2,1,0:T(8,128)(2,1)S(1)} %bitcast_convert_fusion), channel_id=1, replica_groups=mesh['expert'=32,'blk'=8] {'blk'}, dimensions={0} | all-to-all | bytes 1835008 | tf_op jit(solution)/shard_map/all_to_all | solution.py:58
  417.8 1.1 copy.58
  (10 shorter events, 0.2 us)
Async XLA Ops:
  6.5 1.2 copy-start
  6.5 226.1 %all-gather.3.cloned.1.call-start = ((), (), s32[]{:S(2)}) async-start(), calls=%async_computation.3 | async-start | bytes 16515072 | tf_op jit(solution)/shard_map/all_gather | solution.py:43
  65.6 263.6 %all-gather.5.cloned.1.call-start = ((), (), s32[]{:S(2)}) async-start(), calls=%async_computation.4 | async-start | bytes 4718592 | tf_op jit(solution)/shard_map/all_gather | solution.py:45
  232.6 10.4 %copy-start.3 = (bf16[1024,7168]{1,0:T(8,128)(2,1)S(1)}, bf16[1024,7168]{1,0:T(8,128)(2,1)}, u32[]{:S(2)}) copy-start(bf16[1024,7168]{1,0:T(8,128)(2,1)} %all-gather.3.cloned.1.call-done) | copy-start | bytes 44040196
  232.6 11.4 %copy-start.4 = (bf16[1,7168,256]{2,1,0:T(8,128)(2,1)S(1)}, bf16[1,7168,256]{2,1,0:T(8,128)(2,1)}, u32[]{:S(2)}) copy-start(bf16[1,7168,256]{2,1,0:T(8,128)(2,1)} %param.10) | copy-start | bytes 11010052
  341.7 10.6 %copy-start.2 = (bf16[64,8]{0,1:T(8,128)(2,1)S(1)}, bf16[64,8]{0,1:T(8,128)(2,1)}, u32[]{:S(2)}) copy-start(bf16[64,8]{0,1:T(8,128)(2,1)} %param.8) | copy-start | bytes 3076
  341.7 10.6 %copy-start.1 = (s32[64,8]{0,1:T(8,128)S(1)}, s32[64,8]{0,1:T(8,128)}, u32[]{:S(2)}) copy-start(s32[64,8]{0,1:T(8,128)} %param.7) | copy-start | bytes 6148
  343.5 53.4 %all-to-all-start.1 = ((bf16[32,32,896]{2,1,0:T(8,128)(2,1)}), bf16[32,32,896]{2,1,0:T(8,128)(2,1)S(1)}, u32[]{:S(2)}, u32[]{:S(2)}) async-start(bf16[32,32,896]{2,1,0:T(8,128)(2,1)} %copy.53), calls=%async_computation.1 | async-start | bytes 3670016 | tf_op jit(solution)/shard_map/all_to_all | solution.py:52
Sparse Core Ops, SparseCore 0:
  65.7 166.8 all-gather.2
  249.0 80.1 all-gather.4

commit v2 on v1

v2 whole, which is shorter than its diff:
```python
import functools

import jax
import jax.numpy as jnp
from jax import lax
from jax.experimental import pallas as pl
from jax.experimental.pallas import tpu as pltpu
from jax.sharding import PartitionSpec as P

CAP = 4
MESH = pl.DeviceIdType.MESH
STEPS = (0, 1, 7, 2, 6, 3, 5, 4)
NZ = 8
NG = 4
NX = 4
NB = 8
CHUNKS = 4
BF = jnp.bfloat16
F32 = jnp.float32


def slot_tables(id_rows, gate_rows, labels):
    matches = id_rows[:, :, None] == labels[None, None, :]
    chosen = jnp.any(matches, axis=1)
    weights = jnp.sum(jnp.where(matches, gate_rows.astype(F32)[:, :, None], 0.0), axis=1)
    counts = chosen.astype(jnp.int32)
    before = jnp.cumsum(counts, axis=0) - counts
    places = jnp.arange(CAP, dtype=jnp.int32)
    selected = chosen[:, :, None] & (before[:, :, None] == places[None, None, :])
    weighting = jnp.where(selected, weights[:, :, None], 0.0).astype(BF)
    return selected.astype(BF), weighting


def kernel(
    pack_ref, wt_ref, wg_ref, wu_ref, wd_ref, out_ref,
    A, B, X, H, Y, R, PB, OB, WT, WX, WGU, WD, acc, pacc,
    loc, s2s, s2r, s3s, s3r, xs, xr, hs, hr, rs, rr, ws, wr, fs, fr,
):
    e = lax.axis_index("expert")
    b = lax.axis_index("blk")
    z, g = e // NG, e % NG
    yl, co = g // 2, g % 2
    x, yh = b // 2, b % 2
    width = A.shape[-1]

    def expert_at(zz, d):
        return zz * NG + ((yl + d // 2) % 2) * 2 + (co + d % 2) % 2

    def peer(j):
        return (b + j) % NB

    barrier = pltpu.get_barrier_semaphore()
    for i in range(1, NZ * NG):
        pl.semaphore_signal(barrier, inc=1, device_id=((e + i) % (NZ * NG), b), device_id_type=MESH)
    for j in range(1, NB):
        pl.semaphore_signal(barrier, inc=1, device_id=(e, peer(j)), device_id_type=MESH)
    half_w = WGU.shape[1] // 2
    loads = [
        pltpu.make_async_copy(wg_ref, WGU.at[:, pl.ds(0, half_w)], loc.at[0]),
        pltpu.make_async_copy(wu_ref, WGU.at[:, pl.ds(half_w, half_w)], loc.at[1]),
        pltpu.make_async_copy(wd_ref, WD, loc.at[2]),
        pltpu.make_async_copy(wt_ref, WT.at[b], loc.at[3]),
        pltpu.make_async_copy(pack_ref.at[0, 0], A.at[0, 0], loc.at[4]),
        pltpu.make_async_copy(pack_ref.at[1, 0], A.at[1, 0], loc.at[5]),
    ]
    for i in (4, 5, 3, 0, 1, 2):
        loads[i].start()
    pl.semaphore_wait(barrier, NZ * NG - 1 + NB - 1)

    sent = []

    def send(src, dst, ss, rs_, ee, bb):
        copy = pltpu.make_async_remote_copy(
            src_ref=src, dst_ref=dst, send_sem=ss, recv_sem=rs_,
            device_id=(ee, bb), device_id_type=MESH,
        )
        copy.start()
        sent.append(copy)

    def arrived(dst, ss, rs_):
        pltpu.make_async_remote_copy(
            src_ref=dst, dst_ref=dst, send_sem=ss, recv_sem=rs_,
            device_id=(e, peer(1)), device_id_type=MESH,
        ).wait_recv()

    for h in range(2):
        for d in (2, 3, 1):
            send(pack_ref.at[h, d], A.at[h, d], s2s.at[h, d], s2r.at[h, d], expert_at(z, d), b)
    for j in range(1, NB):
        send(wt_ref, WT.at[b], ws.at[j], wr.at[j], e, peer(j))

    def interleave(h):
        loads[4 + h].wait()
        for d in (1, 2, 3):
            arrived(A.at[h, d], s2s.at[h, d], s2r.at[h, d])
        r = lax.broadcasted_iota(jnp.int32, (64, 64), 0)
        c = lax.broadcasted_iota(jnp.int32, (64, 64), 1)
        origin = ((r >> 2) & 3) * 16 + ((r >> 4) & 3) * 4 + (r & 3)
        perm = (c == origin).astype(F32).astype(BF)
        step = 512

        @pl.loop(0, width // step)
        def _(t):
            cols = pl.ds(pl.multiple_of(t * step, step), step)
            rows = A[h, :, :, cols].reshape(64, step)
            moved = jnp.dot(perm, rows, preferred_element_type=F32).astype(BF)
            B[pl.ds(4 * h, 4), :, cols] = moved.reshape(4, 16, step)
            if h == 0:
                X[0, b, pl.ds(0, 16), cols] = moved[:16]

        for i in range(max(1, 4 * h), 4 * h + 4):
            dst = X.at[i // 2, b, pl.ds((i % 2) * 16, 16)]
            send(B.at[i], dst, s3s.at[i], s3r.at[i], ((z + NZ - STEPS[i]) % NZ) * NG + g, b)

    right = ((x + 1) % NX) * 2
    left = ((x + NX - 1) % NX) * 2
    far = ((x + 2) % NX) * 2
    me = x * 2

    class Gather:
        def __init__(self, buf, ss, rsem):
            self.buf, self.ss, self.rs = buf, ss, rsem
            self.half = buf.shape[2] // 2

        def go(self, k, block, slot, to, part=None):
            ref = self.buf.at[k, block]
            if part is not None:
                ref = self.buf.at[k, block, pl.ds(part * self.half, self.half)]
            send(ref, ref, self.ss.at[k, slot], self.rs.at[k, slot], e, to)

        def got(self, k, block, slot, part=None):
            ref = self.buf.at[k, block]
            if part is not None:
                ref = self.buf.at[k, block, pl.ds(part * self.half, self.half)]
            arrived(ref, self.ss.at[k, slot], self.rs.at[k, slot])

        def own(self, k):
            self.go(k, b, 0, right + yh)
            self.go(k, b, 1, left + yh)
            self.go(k, b, 2, me + 1 - yh)

        def partner(self, k):
            self.got(k, me + 1 - yh, 2)
            self.go(k, me + 1 - yh, 3, right + yh)
            self.go(k, me + 1 - yh, 4, left + yh)

        def onward(self, k):
            self.got(k, left + yh, 0)
            self.go(k, left + yh, 5, right + yh, 0)
            self.got(k, right + yh, 1)
            self.go(k, right + yh, 6, left + yh, 1)
            self.got(k, left + 1 - yh, 3)
            self.go(k, left + 1 - yh, 7, right + yh, 0)
            self.got(k, right + 1 - yh, 4)
            self.go(k, right + 1 - yh, 8, left + yh, 1)

        def done(self, k):
            self.got(k, far + yh, 5, 0)
            self.got(k, far + yh, 6, 1)
            self.got(k, far + 1 - yh, 7, 0)
            self.got(k, far + 1 - yh, 8, 1)

    rows_of = Gather(X, xs, xr)
    hidden_of = Gather(H, hs, hr)

    def first(k):
        for i in (2 * k, 2 * k + 1):
            if i:
                arrived(X.at[i // 2, b, pl.ds((i % 2) * 16, 16)], s3s.at[i], s3r.at[i])
        rows_of.own(k)

    def gate_up(k):
        if k == 0:
            loads[0].wait()
            loads[1].wait()
        acc[...] = jnp.zeros_like(acc)
        step = 1024

        @pl.loop(0, width // step)
        def _(t):
            cols = pl.ds(pl.multiple_of(t * step, step), step)
            rows = X[k, :, :, cols].reshape(256, step)
            acc[...] += jnp.dot(rows, WGU[cols, :], preferred_element_type=F32)

        gate, up = acc[:, :half_w], acc[:, half_w:]
        H[k, b] = (gate / (1.0 + jnp.exp(-gate)) * up).astype(BF)

    def down(k):
        if k == 0:
            loads[2].wait()
        n = WD.shape[1]
        r = lax.broadcasted_iota(jnp.int32, (256, 256), 0)
        c = lax.broadcasted_iota(jnp.int32, (256, 256), 1)
        origin = ((r >> 2) & 7) * 32 + ((r >> 7) & 1) * 16 + ((r >> 5) & 3) * 4 + (r & 3)
        perm = (c == origin).astype(F32).astype(BF)
        pacc[pl.ds(0, 256), :] = jnp.zeros((256, n), F32)

        @pl.loop(0, NB)
        def _(q):
            part = WD[pl.ds(pl.multiple_of(q * 256, 256), 256), :]
            pacc[pl.ds(0, 256), :] += jnp.dot(H[k, q], part, preferred_element_type=F32)

        rows = pacc[pl.ds(0, 256), :].astype(BF)
        moved = jnp.dot(perm, rows, preferred_element_type=F32).astype(BF)
        Y[k] = moved.reshape(8, 32, n)
        if k == 0:
            R[0, 0] = moved[:32]
        for q in range(8):
            i, d = 2 * k + q // 4, q % 4
            if i or d:
                send(Y.at[k, q], R.at[k, q], rs.at[k, q], rr.at[k, q], expert_at((z + STEPS[i]) % NZ, d), b)

    def weights():
        loads[3].wait()
        for j in range(1, NB):
            arrived(WT.at[peer(j)], ws.at[j], wr.at[NB - j])
        r = lax.broadcasted_iota(jnp.int32, (128, 1024), 0)
        c = lax.broadcasted_iota(jnp.int32, (128, 1024), 1)
        same = r == ((c >> 5) * 4 + (c & 3))

        @pl.loop(0, NB)
        def _(q):
            spread = jnp.where(same & (((c >> 2) & 7) == q), 1.0, 0.0).astype(BF)
            wide = jnp.dot(WT[q], spread, preferred_element_type=F32).astype(BF)
            WX[pl.ds(pl.multiple_of(q * 64, 64), 64), :] = wide

    def combine(k):
        for q in range(8):
            if k or q:
                arrived(R.at[k, q], rs.at[k, q], rr.at[k, q])
        n = WD.shape[1]
        part = WX[:, k * 256 : (k + 1) * 256]
        term = jnp.dot(part, R[k].reshape(256, n), preferred_element_type=F32)
        if k == 0:
            pacc[...] = term
        else:
            pacc[...] += term

    interleave(0)
    first(0)
    interleave(1)
    first(1)
    rows_of.partner(0)
    rows_of.onward(0)
    rows_of.partner(1)
    first(2)
    weights()
    for k in range(CHUNKS):
        rows_of.done(k)
        gate_up(k)
        hidden_of.own(k)
        if k + 1 < CHUNKS:
            rows_of.onward(k + 1)
        if k + 2 < CHUNKS:
            rows_of.partner(k + 2)
        if k + 3 < CHUNKS:
            first(k + 3)
        hidden_of.partner(k)
        hidden_of.onward(k)
        if k:
            hidden_of.done(k - 1)
            down(k - 1)
    hidden_of.done(CHUNKS - 1)
    down(CHUNKS - 1)
    for k in range(CHUNKS):
        combine(k)
    for q in range(NB):
        PB[q] = pacc[q * 64 : (q + 1) * 64, :].astype(BF)
    for j in range(1, NB):
        send(PB.at[peer(j)], OB.at[b], fs.at[j], fr.at[j], e, peer(j))
    OB[b] = PB[b]
    for j in range(1, NB):
        arrived(OB.at[peer(j)], fs.at[j], fr.at[NB - j])
    n = WD.shape[1]
    for q in range(NB):
        out_ref[:, q * n : (q + 1) * n] = OB[q]
    for copy in sent:
        copy.wait_send()


def on_device(tokens, expert_ids, gate_weights, w_gate, w_up, w_down):
    tok, width = tokens.shape
    half_w = w_gate.shape[2]
    full_w, n = w_down.shape[1:]
    e = lax.axis_index("expert")
    z, g = e // NG, e % NG
    steps = jnp.array(STEPS, jnp.int32)
    d = jnp.arange(NG, dtype=jnp.int32)
    quad = ((g // 2 + d // 2) % 2) * 2 + (g % 2 + d % 2) % 2
    labels = (((z + NZ - steps) % NZ)[:, None] * NG + quad[None, :]).reshape(-1)
    selector, weighting = slot_tables(expert_ids, gate_weights, labels)
    selector = selector.reshape(tok, 2, 4, NG, CAP).transpose(1, 3, 2, 4, 0).reshape(128, tok)
    packed = jnp.dot(selector, tokens, preferred_element_type=F32).astype(BF)
    packed = packed.reshape(2, NG, 16, width)
    weighting = weighting.reshape(tok, 128)
    dma = pltpu.SemaphoreType.DMA
    any_ = pl.BlockSpec(memory_space=pl.ANY)
    return pl.pallas_call(
        kernel,
        out_shape=jax.ShapeDtypeStruct((tok, width), BF),
        in_specs=[any_] * 5,
        out_specs=pl.BlockSpec(memory_space=pltpu.VMEM),
        scratch_shapes=[
            pltpu.VMEM((2, NG, 16, width), BF),
            pltpu.VMEM((NZ, 16, width), BF),
            pltpu.VMEM((CHUNKS, NB, 32, width), BF),
            pltpu.VMEM((CHUNKS, NB, 256, half_w), BF),
            pltpu.VMEM((CHUNKS, 8, 32, n), BF),
            pltpu.VMEM((CHUNKS, 8, 32, n), BF),
            pltpu.VMEM((NB, tok, n), BF),
            pltpu.VMEM((NB, tok, n), BF),
            pltpu.VMEM((NB, tok, 128), BF),
            pltpu.VMEM((NB * tok, 1024), BF),
            pltpu.VMEM((width, 2 * half_w), BF),
            pltpu.VMEM((full_w, n), BF),
            pltpu.VMEM((256, 2 * half_w), F32),
            pltpu.VMEM((NB * tok, n), F32),
            dma((6,)),
            dma((2, NG)), dma((2, NG)),
            dma((NZ,)), dma((NZ,)),
            dma((CHUNKS, 9)), dma((CHUNKS, 9)),
            dma((CHUNKS, 9)), dma((CHUNKS, 9)),
            dma((CHUNKS, 8)), dma((CHUNKS, 8)),
            dma((NB,)), dma((NB,)),
            dma((NB,)), dma((NB,)),
        ],
        compiler_params=pltpu.CompilerParams(
            collective_id=0, has_side_effects=True, vmem_limit_bytes=60 * 1024 * 1024
        ),
    )(packed, weighting, w_gate[0], w_up[0], w_down[0])


def solution(mesh):
    return jax.shard_map(
        on_device,
        mesh=mesh,
        in_specs=(
            P(("expert", "blk"), None),
            P(("expert", "blk"), None),
            P(("expert", "blk"), None),
            P("expert", None, "blk"),
            P("expert", None, "blk"),
            P("expert", None, "blk"),
        ),
        out_specs=P(("expert", "blk"), None),
        check_vma=False,
    )
```

time: 427 us -> 276 us (0.65)
  Pallas kernels: 0 us -> 259 us
  waiting for transfers between devices: 257 us -> 0 us
  blocking collectives: 108 us -> 0 us
  matrix products: 23.8 us -> 1.94 us
  between operations: 13.6 us -> 0.14 us
  other arithmetic: 0.99 us -> 10.3 us
  local copies, waits for them, and re-layouts: 13.3 us -> 4.42 us
  starting transfers between devices: 8.77 us -> 0 us
    pallas_call x0 -> x1, Pallas kernels: none -> 259 us  [on_device(): pl.pallas_call(kernel, out_shape=jax.ShapeDtypeStruct((tok, width), BF),...]
    all_gather x2 -> x0, waiting for transfers between devices: 247 us -> none  [the longest x1 167 us: on_device(): row_block = lax.all_gather(mine, 'blk', axis=0, tiled=True)]
    all_to_all x2 -> x0, blocking collectives: 74.1 us -> none  [the longest x1 54.3 us: on_device(): lax.all_to_all(outgoing, 'expert', split_axis=0, concat_axis=0, tiled=True)]
    all_gather x1 -> x0, blocking collectives: 34.3 us -> none  [on_device(): lax.all_gather(weighting.reshape(tok_dev, experts * CAP), 'blk', axis=0,...]
    dot_general x5 -> x1, matrix products: 23.8 us -> 1.94 us  [on_device(): packed = jnp.dot(selector, tokens, preferred_element_type=F32).astype(BF)]
    all_to_all x1 -> x0, waiting for transfers between devices: 9.7 us -> none  [on_device(): lax.all_to_all(slices, 'expert', split_axis=0, concat_axis=0, tiled=True)]
    all_to_all x1 -> x0, starting transfers between devices: 8.54 us -> none  [on_device(): lax.all_to_all(slices, 'expert', split_axis=0, concat_axis=0, tiled=True)]
    reshape x5 -> x0, local copies, waits for them, and re-layouts: 6.86 us -> none  [the longest x2 3.41 us: on_device(): slices = slices.reshape(blocks, experts, CAP, -1).transpose(1, 0, 2, 3)]
  transfers between devices with their start and end apart: 3 -> 0, of which waited for: 3 -> 0; matrix products, arithmetic and copies ran while one was open for 0% -> 0% of each run, Pallas kernels for 0% -> 0%
where the time goes in v2:
time: 276 us
  Pallas kernels  259 us (94%)
  other arithmetic  10.3 us (4%)
  local copies, waits for them, and re-layouts  4.42 us (2%)
    pallas_call x1, Pallas kernels, on_device(): pl.pallas_call(kernel, out_shape=jax.ShapeDtypeStruct((tok, width), BF),...  259 us
    another operation x1, other arithmetic, slot_tables(): before = jnp.cumsum(counts, axis=0) - counts  6.6 us

profile of v2, /device:TPU:56, one launch (start us, length us, event | category | flops | bytes accessed | tf_op | source)
XLA Modules:
  0.0 275.9 jit_solution(918327223143550315)
XLA Ops:
  0.0 0.0 copy-start
  0.0 0.7 fusion.7
  0.8 0.1 broadcast_add_fusion
  0.8 0.1 add.111
  0.9 0.8 compare_reduce_fusion
  1.7 0.7 convert_element_type.36
  2.4 0.8 fusion
  3.2 0.1 copy.29
  3.4 0.1 eq.72
  3.5 0.1 eq.66
  3.6 0.1 copy.30
  3.7 1.0 copy.24
  4.7 6.6 %fusion.12 = s32[64,32,1]{2,1,0:T(8,128)S(1)} fusion(s32[64,32,1]{2,1,0:T(8,128)S(1)} %copy.24), kind=kOutput, calls=%fused_computation.34 | output fusion | flops 129024 | bytes 16384 | tf_op jit(solution)/shard_map/jit(cumsum)/reduce_window_sum | solution.py:27
  11.3 0.6 copy.25
  12.0 0.1 copy.28
  12.0 0.6 select_convert_fusion.wt_ref
  12.7 0.0 copy-done
  12.7 1.9 convolution_convert_fusion
  14.7 259.1 %shard_map.73 = bf16[64,7168]{1,0:T(8,128)(2,1)} custom-call(bf16[2,4,16,7168]{3,2,1,0:T(8,128)(2,1)} %bitcast.21, bf16[64,128]{1,0:T(8,128)(2,1)} %select_convert_fusion.wt_ref, bf16[7168,256]{1,0:T(8,128)(2,1)} %bitcast.22, bf16[7168,256]{1,0:T(8,128)(2,1)} %bitcast.23, bf16[2048,896]{1,0:T(8,128)(2,1)} %bitcast.24), custom_call_target="tpu_custom_call" | custom-call | tf_op jit(solution)/shard_map/pallas_call | solution.py:298
  273.7 2.2 copy.32
  (13 shorter events, 0.1 us)
Async XLA Ops:
  0.0 12.7 %copy-start = (bf16[64,7168]{1,0:T(8,128)(2,1)S(1)}, bf16[64,7168]{1,0:T(8,128)(2,1)}, u32[]{:S(2)}) copy-start(bf16[64,7168]{1,0:T(8,128)(2,1)} %param.7) | copy-start | bytes 2752516

commit v3 on v1

v3 whole, which is shorter than its diff:
```python
import functools

import jax
import jax.numpy as jnp
from jax import lax
from jax.experimental import pallas as pl
from jax.experimental.pallas import tpu as pltpu
from jax.sharding import PartitionSpec as P

CAP = 4
MESH = pl.DeviceIdType.MESH
STEPS = (0, 2, 4, 5, 3, 6, 1, 7)
XFIRST = (2, 4)
CHUNKS = ((0, 2), (2, 2), (4, 2), (6, 1), (7, 1))
DIRECT = (3, 4)
NZ = 8
NG = 4
NX = 4
NB = 8
BF = jnp.bfloat16
F32 = jnp.float32


def kernel(
    tok_ref, ids_ref, gw_ref, wg_ref, wu_ref, wd_ref, out_ref,
    TK, IDS, GW, O, A, B, X, H, Y, R, PB, OB, WO, WT, WX, WGU, WD, acc, pacc,
    loc, s2s, s2r, s3s, s3r, xs, xr, hs, hr, rs, rr, ws, wr, fs, fr,
):
    e = lax.axis_index("expert")
    b = lax.axis_index("blk")
    z, g = e // NG, e % NG
    yl, co = g // 2, g % 2
    x, yh = b // 2, b % 2
    width = A.shape[-1]
    half_c = width // 2
    half_w = WGU.shape[1] // 2
    n = WD.shape[1]

    def expert_at(zz, d):
        return zz * NG + ((yl + d // 2) % 2) * 2 + (co + d % 2) % 2

    def peer(j):
        return (b + j) % NB

    barrier = pltpu.get_barrier_semaphore()
    loads = [
        pltpu.make_async_copy(ids_ref, IDS, loc.at[0]),
        pltpu.make_async_copy(gw_ref, GW, loc.at[1]),
        pltpu.make_async_copy(tok_ref, TK, loc.at[2]),
        pltpu.make_async_copy(wg_ref, WGU.at[:, pl.ds(0, half_w)], loc.at[3]),
        pltpu.make_async_copy(wu_ref, WGU.at[:, pl.ds(half_w, half_w)], loc.at[4]),
        pltpu.make_async_copy(wd_ref, WD, loc.at[5]),
    ]
    for copy in loads:
        copy.start()
    for i in range(1, NZ * NG):
        pl.semaphore_signal(barrier, inc=1, device_id=((e + i) % (NZ * NG), b), device_id_type=MESH)
    for j in range(1, NB):
        pl.semaphore_signal(barrier, inc=1, device_id=(e, peer(j)), device_id_type=MESH)

    def label_of(unit, d):
        step = sum(jnp.where(unit == i, s, 0) for i, s in enumerate(STEPS))
        return ((z + NZ - step) & 7) * NG + ((yl + (d >> 1)) & 1) * 2 + ((co + d) & 1)

    def chosen_of(labels, place):
        ids = IDS[...]
        gate = GW[...].astype(F32)
        hit = jnp.zeros((ids.shape[0], 128), F32)
        weight = jnp.zeros((ids.shape[0], 128), F32)
        for j in range(ids.shape[1]):
            match = ids[:, j : j + 1] == labels
            hit = jnp.where(match, 1.0, hit)
            weight = jnp.where(match, gate[:, j : j + 1], weight)
        r = lax.broadcasted_iota(jnp.int32, (ids.shape[0], ids.shape[0]), 0)
        c = lax.broadcasted_iota(jnp.int32, (ids.shape[0], ids.shape[0]), 1)
        earlier = jnp.where(c < r, 1.0, 0.0).astype(BF)
        before = jnp.dot(earlier, hit.astype(BF), preferred_element_type=F32)
        used = (hit > 0.5) & (before == place.astype(F32))
        return jnp.where(used, 1.0, 0.0), jnp.where(used, weight, 0.0)

    loads[0].wait()
    loads[1].wait()
    col = lax.broadcasted_iota(jnp.int32, (1, 128), 1)
    selector, _ = chosen_of(label_of((col >> 6) * 4 + ((col >> 2) & 3), (col >> 4) & 3), col & 3)
    selector = selector.T.astype(BF)
    _, weighting = chosen_of(label_of(col >> 4, (col >> 2) & 3), col & 3)
    WO[...] = weighting.astype(BF)
    WT[b] = weighting.astype(BF)
    loads[2].wait()

    def pack(h, c):
        step = 512

        @pl.loop(0, half_c // step)
        def _(t):
            cols = pl.ds(pl.multiple_of(c * half_c + t * step, step), step)
            rows = jnp.dot(selector[h * 64 : h * 64 + 64], TK[:, cols], preferred_element_type=F32)
            rows = rows.astype(BF).reshape(NG, 16, step)
            O[h, :, :, cols] = rows
            A[h, 0, :, cols] = rows[0]

    for h in range(2):
        for c in range(2):
            pack(h, c)
    pl.semaphore_wait(barrier, NZ * NG - 1 + NB - 1)

    sent = []

    def send(src, dst, ss, rs_, ee, bb):
        copy = pltpu.make_async_remote_copy(
            src_ref=src, dst_ref=dst, send_sem=ss, recv_sem=rs_,
            device_id=(ee, bb), device_id_type=MESH,
        )
        copy.start()
        sent.append(copy)

    def arrived(dst, ss, rs_):
        pltpu.make_async_remote_copy(
            src_ref=dst, dst_ref=dst, send_sem=ss, recv_sem=rs_,
            device_id=(e, peer(1)), device_id_type=MESH,
        ).wait_recv()

    def side(c):
        return pl.ds(c * half_c, half_c)

    for h in range(2):
        for c in range(2):
            for d in (2, 3, 1):
                send(
                    O.at[h, d, :, side(c)], A.at[h, d, :, side(c)],
                    s2s.at[h, c, d], s2r.at[h, c, d], expert_at(z, d), b,
                )

    def interleave(h, c):
        for d in (1, 2, 3):
            arrived(A.at[h, d, :, side(c)], s2s.at[h, c, d], s2r.at[h, c, d])
        r = lax.broadcasted_iota(jnp.int32, (64, 64), 0)
        q = lax.broadcasted_iota(jnp.int32, (64, 64), 1)
        origin = ((r >> 2) & 3) * 16 + ((r >> 4) & 3) * 4 + (r & 3)
        perm = (q == origin).astype(F32).astype(BF)
        step = 512

        @pl.loop(0, half_c // step)
        def _(t):
            cols = pl.ds(pl.multiple_of(c * half_c + t * step, step), step)
            rows = A[h, :, :, cols].reshape(64, step)
            moved = jnp.dot(perm, rows, preferred_element_type=F32).astype(BF)
            B[pl.ds(4 * h, 4), :, cols] = moved.reshape(4, 16, step)
            if h == 0:
                X[0, b, :, cols] = moved[:16]

    def along_z(h):
        for i in range(max(1, 4 * h), 4 * h + 4):
            send(
                B.at[i], X.at[i, b], s3s.at[i], s3r.at[i],
                ((z + NZ - STEPS[i]) % NZ) * NG + g, b,
            )

    right = ((x + 1) % NX) * 2
    left = ((x + NX - 1) % NX) * 2
    far = ((x + 2) % NX) * 2
    me = x * 2
    other = 1 - yh

    def go(i, block, slot, to, c=None):
        ref = X.at[i, block] if c is None else X.at[i, block, :, side(c)]
        send(ref, ref, xs.at[i, slot], xr.at[i, slot], e, to)

    def got(i, block, slot, c=None):
        ref = X.at[i, block] if c is None else X.at[i, block, :, side(c)]
        arrived(ref, xs.at[i, slot], xr.at[i, slot])

    def own_side(i, c):
        go(i, b, 0 + c, right + yh, c)
        go(i, b, 2 + c, left + yh, c)
        if i not in XFIRST:
            go(i, b, 4 + c, me + other, c)

    def own(i):
        arrived(X.at[i, b], s3s.at[i], s3r.at[i])
        if i in XFIRST:
            go(i, b, 4, me + other)
        go(i, b, 0, right + yh, 0)
        go(i, b, 3, left + yh, 1)
        if i not in XFIRST:
            go(i, b, 4, me + other, 0)
            go(i, b, 5, me + other, 1)
        go(i, b, 1, right + yh, 1)
        go(i, b, 2, left + yh, 0)

    def part(i):
        if i in XFIRST:
            return
        got(i, me + other, 4, 0)
        go(i, me + other, 6, right + other_row, 0)
        got(i, me + other, 5, 1)
        go(i, me + other, 9, left + other_row, 1)
        go(i, me + other, 7, right + other_row, 1)
        go(i, me + other, 8, left + other_row, 0)

    other_row = yh

    def onward(i):
        got(i, left + yh, 0, 0)
        go(i, left + yh, 10, right + yh, 0)
        got(i, right + yh, 3, 1)
        go(i, right + yh, 11, left + yh, 1)
        if i in XFIRST:
            got(i, left + yh, 1, 1)
            go(i, left + yh, 5, me + other)
            got(i, right + yh, 2, 0)
            go(i, right + yh, 6, me + other)
        else:
            got(i, left + other, 6, 0)
            go(i, left + other, 12, right + yh, 0)
            got(i, right + other, 9, 1)
            go(i, right + other, 13, left + yh, 1)

    def done(i):
        got(i, far + yh, 10, 0)
        got(i, far + yh, 11, 1)
        if i in XFIRST:
            go(i, far + yh, 7, me + other)
            got(i, me + other, 4)
            got(i, left + other, 5)
            got(i, right + other, 6)
            got(i, far + other, 7)
        else:
            got(i, left + yh, 1, 1)
            got(i, right + yh, 2, 0)
            got(i, left + other, 7, 1)
            got(i, right + other, 8, 0)
            got(i, far + other, 12, 0)
            got(i, far + other, 13, 1)

    def h_ref(k, block, part_=None):
        i0, m = CHUNKS[k]
        if part_ is None:
            return H.at[pl.ds(i0, m), block]
        return H.at[pl.ds(i0, m), block, pl.ds(part_ * 64, 64)]

    def h_go(k, block, slot, to, part_=None):
        ref = h_ref(k, block, part_)
        send(ref, ref, hs.at[k, slot], hr.at[k, slot], e, to)

    def h_got(k, block, slot, part_=None):
        arrived(h_ref(k, block, part_), hs.at[k, slot], hr.at[k, slot])

    def h_own(k):
        if k in DIRECT:
            for j in (4, 3, 5, 2, 6, 1, 7):
                h_go(k, b, j, peer(j))
            return
        h_go(k, b, 2, me + other)
        h_go(k, b, 0, right + yh)
        h_go(k, b, 1, left + yh)

    def h_part(k):
        if k in DIRECT:
            return
        h_got(k, me + other, 2)
        h_go(k, me + other, 3, right + yh)
        h_go(k, me + other, 4, left + yh)

    def h_onward(k):
        if k in DIRECT:
            return
        h_got(k, left + yh, 0)
        h_go(k, left + yh, 5, right + yh, 0)
        h_got(k, right + yh, 1)
        h_go(k, right + yh, 6, left + yh, 1)
        h_got(k, left + other, 3)
        h_go(k, left + other, 7, right + yh, 0)
        h_got(k, right + other, 4)
        h_go(k, right + other, 8, left + yh, 1)

    def h_done(k):
        if k in DIRECT:
            for j in range(1, NB):
                h_got(k, peer(j), NB - j)
            return
        h_got(k, far + yh, 5, 0)
        h_got(k, far + yh, 6, 1)
        h_got(k, far + other, 7, 0)
        h_got(k, far + other, 8, 1)

    def gate_up(k):
        if k == 0:
            loads[3].wait()
            loads[4].wait()
        i0, m = CHUNKS[k]
        size = m * 128
        step = 1792

        @pl.loop(0, width // step)
        def _(t):
            cols = pl.ds(pl.multiple_of(t * step, step), step)
            rows = X[i0 : i0 + m, :, :, cols].reshape(size, step)
            term = jnp.dot(rows, WGU[cols, :], preferred_element_type=F32)

            @pl.when(t == 0)
            def _():
                acc[:size] = term

            @pl.when(t > 0)
            def _():
                acc[:size] += term

        gate, up = acc[:size, :half_w], acc[:size, half_w:]
        hidden = (gate / (1.0 + jnp.exp(-gate)) * up).astype(BF)
        H[i0 : i0 + m, b] = hidden.reshape(m, 128, half_w)

    def down(k):
        if k == 0:
            loads[5].wait()
        i0, m = CHUNKS[k]
        size = m * 128
        r = lax.broadcasted_iota(jnp.int32, (128, 128), 0)
        c = lax.broadcasted_iota(jnp.int32, (128, 128), 1)
        origin = ((r >> 2) & 7) * 16 + ((r >> 5) & 3) * 4 + (r & 3)
        perm = (c == origin).astype(F32).astype(BF)
        total = None
        for q in range(NB):
            term = jnp.dot(
                H[i0 : i0 + m, q].reshape(size, half_w),
                WD[q * half_w : (q + 1) * half_w, :],
                preferred_element_type=F32,
            )
            total = term if total is None else total + term
        rows = total.astype(BF)
        for u in range(m):
            i = i0 + u
            moved = jnp.dot(perm, rows[u * 128 : (u + 1) * 128], preferred_element_type=F32).astype(BF)
            Y[i] = moved.reshape(NG, 32, n)
            if i == 0:
                R[0, 0] = moved[:32]
            for d in (3, 2, 1, 0):
                if i or d:
                    send(
                        Y.at[i, d], R.at[i, d], rs.at[i, d], rr.at[i, d],
                        expert_at((z + STEPS[i]) % NZ, d), b,
                    )

    def weights():
        for j in range(1, NB):
            arrived(WT.at[peer(j)], ws.at[j], wr.at[NB - j])
        r = lax.broadcasted_iota(jnp.int32, (128, 1024), 0)
        c = lax.broadcasted_iota(jnp.int32, (128, 1024), 1)
        same = r == ((c >> 5) * 4 + (c & 3))

        @pl.loop(0, NB)
        def _(q):
            spread = jnp.where(same & (((c >> 2) & 7) == q), 1.0, 0.0).astype(BF)
            wide = jnp.dot(WT[q], spread, preferred_element_type=F32).astype(BF)
            WX[pl.ds(pl.multiple_of(q * 64, 64), 64), :] = wide

    def combine(k):
        i0, m = CHUNKS[k]
        for i in range(i0, i0 + m):
            for d in range(NG):
                if i or d:
                    arrived(R.at[i, d], rs.at[i, d], rr.at[i, d])
        part_ = WX[:, i0 * 128 : (i0 + m) * 128]
        term = jnp.dot(part_, R[i0 : i0 + m].reshape(m * 128, n), preferred_element_type=F32)
        if k == 0:
            pacc[...] = term
        elif k + 1 < len(CHUNKS):
            pacc[...] += term
        else:
            PB[...] = (pacc[...] + term).astype(BF).reshape(NB, 64, n)

    interleave(0, 0)
    own_side(0, 0)
    interleave(0, 1)
    own_side(0, 1)
    along_z(0)
    for j in range(1, NB):
        send(WO, WT.at[b], ws.at[j], wr.at[j], e, peer(j))
    part(0)
    interleave(1, 0)
    interleave(1, 1)
    along_z(1)
    own(1)
    onward(0)
    part(1)
    own(2)
    weights()
    for t in range(1, 9):
        if t + 2 < 8:
            own(t + 2)
        if t + 1 < 8:
            part(t + 1)
        if t < 8:
            onward(t)
        if t == 3:
            h_part(0)
        if t == 5:
            h_part(1)
        if t == 7:
            h_part(2)
        done(t - 1)
        if t == 2:
            gate_up(0)
            h_own(0)
        if t == 3:
            h_onward(0)
        if t == 4:
            gate_up(1)
            h_own(1)
            h_done(0)
            down(0)
        if t == 5:
            h_onward(1)
        if t == 6:
            gate_up(2)
            h_own(2)
            h_done(1)
            down(1)
            combine(0)
        if t == 7:
            h_onward(2)
            gate_up(3)
            h_own(3)
        if t == 8:
            gate_up(4)
            h_own(4)
            h_done(2)
            down(2)
            h_done(3)
            down(3)
            h_done(4)
            down(4)
    for k in range(1, 5):
        combine(k)
    for j in (4, 3, 5, 2, 6, 1, 7):
        send(PB.at[peer(j)], OB.at[b], fs.at[j], fr.at[j], e, peer(j))
    OB[b] = PB[b]
    for j in range(1, NB):
        arrived(OB.at[peer(j)], fs.at[j], fr.at[NB - j])
    for q in range(NB):
        out_ref[:, q * n : (q + 1) * n] = OB[q]
    for copy in sent:
        copy.wait_send()


def on_device(tokens, expert_ids, gate_weights, w_gate, w_up, w_down):
    tok, width = tokens.shape
    half_w = w_gate.shape[2]
    full_w, n = w_down.shape[1:]
    dma = pltpu.SemaphoreType.DMA
    any_ = pl.BlockSpec(memory_space=pl.ANY)
    units = NZ
    return pl.pallas_call(
        kernel,
        out_shape=jax.ShapeDtypeStruct((tok, width), BF),
        in_specs=[any_] * 6,
        out_specs=pl.BlockSpec(memory_space=pltpu.VMEM),
        scratch_shapes=[
            pltpu.VMEM((tok, width), BF),
            pltpu.VMEM(expert_ids.shape, jnp.int32),
            pltpu.VMEM(gate_weights.shape, BF),
            pltpu.VMEM((2, NG, 16, width), BF),
            pltpu.VMEM((2, NG, 16, width), BF),
            pltpu.VMEM((units, 16, width), BF),
            pltpu.VMEM((units, NB, 16, width), BF),
            pltpu.VMEM((units, NB, 128, half_w), BF),
            pltpu.VMEM((units, NG, 32, n), BF),
            pltpu.VMEM((units, NG, 32, n), BF),
            pltpu.VMEM((NB, tok, n), BF),
            pltpu.VMEM((NB, tok, n), BF),
            pltpu.VMEM((tok, 128), BF),
            pltpu.VMEM((NB, tok, 128), BF),
            pltpu.VMEM((NB * tok, 1024), BF),
            pltpu.VMEM((width, 2 * half_w), BF),
            pltpu.VMEM((full_w, n), BF),
            pltpu.VMEM((256, 2 * half_w), F32),
            pltpu.VMEM((NB * tok, n), F32),
            dma((6,)),
            dma((2, 2, NG)), dma((2, 2, NG)),
            dma((units,)), dma((units,)),
            dma((units, 14)), dma((units, 14)),
            dma((len(CHUNKS), 9)), dma((len(CHUNKS), 9)),
            dma((units, NG)), dma((units, NG)),
            dma((NB,)), dma((NB,)),
            dma((NB,)), dma((NB,)),
        ],
        compiler_params=pltpu.CompilerParams(
            collective_id=0, has_side_effects=True, vmem_limit_bytes=63 * 1024 * 1024
        ),
    )(tokens, expert_ids, gate_weights, w_gate[0], w_up[0], w_down[0])


def solution(mesh):
    return jax.shard_map(
        on_device,
        mesh=mesh,
        in_specs=(
            P(("expert", "blk"), None),
            P(("expert", "blk"), None),
            P(("expert", "blk"), None),
            P("expert", None, "blk"),
            P("expert", None, "blk"),
            P("expert", None, "blk"),
        ),
        out_specs=P(("expert", "blk"), None),
        check_vma=False,
    )
```

time: 427 us -> 217 us (0.51)
  waiting for transfers between devices: 257 us -> 0 us
  Pallas kernels: 0 us -> 209 us
  blocking collectives: 108 us -> 0 us
  matrix products: 23.8 us -> 0 us
  between operations: 13.6 us -> 0.01 us
  starting transfers between devices: 8.77 us -> 0 us
  local copies, waits for them, and re-layouts: 13.3 us -> 4.91 us
    all_gather x2 -> x0, waiting for transfers between devices: 247 us -> none  [the longest x1 167 us: on_device(): row_block = lax.all_gather(mine, 'blk', axis=0, tiled=True)]
    pallas_call x0 -> x1, Pallas kernels: none -> 209 us  [on_device(): pl.pallas_call(kernel, out_shape=jax.ShapeDtypeStruct((tok, width), BF),...]
    all_to_all x2 -> x0, blocking collectives: 74.1 us -> none  [the longest x1 54.3 us: on_device(): lax.all_to_all(outgoing, 'expert', split_axis=0, concat_axis=0, tiled=True)]
    all_gather x1 -> x0, blocking collectives: 34.3 us -> none  [on_device(): lax.all_gather(weighting.reshape(tok_dev, experts * CAP), 'blk', axis=0,...]
    dot_general x5 -> x0, matrix products: 23.8 us -> none  [the longest x1 9.07 us: on_device(): jnp.dot(hidden_all, down_mat, preferred_element_type=jnp.float32)]
    all_to_all x1 -> x0, waiting for transfers between devices: 9.7 us -> none  [on_device(): lax.all_to_all(slices, 'expert', split_axis=0, concat_axis=0, tiled=True)]
    all_to_all x1 -> x0, starting transfers between devices: 8.54 us -> none  [on_device(): lax.all_to_all(slices, 'expert', split_axis=0, concat_axis=0, tiled=True)]
    reshape x5 -> x0, local copies, waits for them, and re-layouts: 6.86 us -> none  [the longest x2 3.41 us: on_device(): slices = slices.reshape(blocks, experts, CAP, -1).transpose(1, 0, 2, 3)]
  transfers between devices with their start and end apart: 3 -> 0, of which waited for: 3 -> 0; matrix products, arithmetic and copies ran while one was open for 0% -> 0% of each run, Pallas kernels for 0% -> 0%
where the time goes in v3:
time: 217 us; the launch traced here: 214 us
  Pallas kernels  209 us (96%)
  local copies, waits for them, and re-layouts  4.91 us (2%)
    pallas_call x1, Pallas kernels, on_device(): pl.pallas_call(kernel, out_shape=jax.ShapeDtypeStruct((tok, width), BF),...  209 us
    unnamed x3, local copies, waits for them, and re-layouts  4.91 us

profile of v3, /device:TPU:56, one launch (start us, length us, event | category | flops | bytes accessed | tf_op | source)
XLA Modules:
  0.0 213.6 jit_solution(12244057164811119761)
XLA Ops:
  0.0 1.4 copy.8.gw_ref
  1.4 1.4 copy.7.ids_ref
  2.7 208.7 %shard_map.64 = bf16[64,7168]{1,0:T(8,128)(2,1)} custom-call(bf16[64,7168]{1,0:T(8,128)(2,1)} %tok_ref.1, s32[64,8]{1,0:T(8,128)} %copy.7.ids_ref, bf16[64,8]{1,0:T(8,128)(2,1)} %copy.8.gw_ref, bf16[7168,256]{1,0:T(8,128)(2,1)} %bitcast.3, bf16[7168,256]{1,0:T(8,128)(2,1)} %bitcast.4, bf16[2048,896]{1,0:T(8,128)(2,1)} %bitcast.5), custom_call_target="tpu_custom_call" | custom-call | tf_op jit(solution)/shard_map/pallas_call | solution.py:453
  211.5 2.2 %copy.10 = bf16[64,7168]{1,0:T(8,128)(2,1)} copy(bf16[64,7168]{1,0:T(8,128)(2,1)} %shard_map.64) | data formatting | bytes 1835008

commit v4 on v3

--- a/solution.py
+++ b/solution.py
@@ -9,7 +9,7 @@
 
 CAP = 4
 MESH = pl.DeviceIdType.MESH
-STEPS = (0, 2, 4, 5, 3, 6, 1, 7)
+STEPS = (0, 1, 4, 5, 3, 6, 2, 7)
 XFIRST = (2, 4)
 CHUNKS = ((0, 2), (2, 2), (4, 2), (6, 1), (7, 1))
 DIRECT = (3, 4)
@@ -51,12 +51,15 @@
         pltpu.make_async_copy(wu_ref, WGU.at[:, pl.ds(half_w, half_w)], loc.at[4]),
         pltpu.make_async_copy(wd_ref, WD, loc.at[5]),
     ]
-    for copy in loads:
+    for copy in loads[:3]:
         copy.start()
-    for i in range(1, NZ * NG):
-        pl.semaphore_signal(barrier, inc=1, device_id=((e + i) % (NZ * NG), b), device_id_type=MESH)
-    for j in range(1, NB):
-        pl.semaphore_signal(barrier, inc=1, device_id=(e, peer(j)), device_id_type=MESH)
+    for d in range(1, NG):
+        pl.semaphore_signal(barrier, inc=1, device_id=(expert_at(z, d), b), device_id_type=MESH)
+    for i in range(1, NZ):
+        pl.semaphore_signal(barrier, inc=1, device_id=((z + i) % NZ * NG + g, b), device_id_type=MESH)
+    near = (((x + 1) % NX) * 2 + yh, ((x + NX - 1) % NX) * 2 + yh, x * 2 + 1 - yh)
+    for block in near:
+        pl.semaphore_signal(barrier, inc=1, device_id=(e, block), device_id_type=MESH)
 
     def label_of(unit, d):
         step = sum(jnp.where(unit == i, s, 0) for i, s in enumerate(STEPS))
@@ -65,27 +68,25 @@
     def chosen_of(labels, place):
         ids = IDS[...]
         gate = GW[...].astype(F32)
-        hit = jnp.zeros((ids.shape[0], 128), F32)
-        weight = jnp.zeros((ids.shape[0], 128), F32)
-        for j in range(ids.shape[1]):
-            match = ids[:, j : j + 1] == labels
+        tok = ids.shape[1]
+        hit = jnp.zeros((128, tok), F32)
+        weight = jnp.zeros((128, tok), F32)
+        for j in range(ids.shape[0]):
+            match = ids[j : j + 1] == labels
             hit = jnp.where(match, 1.0, hit)
-            weight = jnp.where(match, gate[:, j : j + 1], weight)
-        r = lax.broadcasted_iota(jnp.int32, (ids.shape[0], ids.shape[0]), 0)
-        c = lax.broadcasted_iota(jnp.int32, (ids.shape[0], ids.shape[0]), 1)
-        earlier = jnp.where(c < r, 1.0, 0.0).astype(BF)
-        before = jnp.dot(earlier, hit.astype(BF), preferred_element_type=F32)
+            weight = jnp.where(match, gate[j : j + 1], weight)
+        r = lax.broadcasted_iota(jnp.int32, (tok, tok), 0)
+        c = lax.broadcasted_iota(jnp.int32, (tok, tok), 1)
+        earlier = jnp.where(r < c, 1.0, 0.0).astype(BF)
+        before = jnp.dot(hit.astype(BF), earlier, preferred_element_type=F32)
         used = (hit > 0.5) & (before == place.astype(F32))
         return jnp.where(used, 1.0, 0.0), jnp.where(used, weight, 0.0)
 
     loads[0].wait()
     loads[1].wait()
-    col = lax.broadcasted_iota(jnp.int32, (1, 128), 1)
-    selector, _ = chosen_of(label_of((col >> 6) * 4 + ((col >> 2) & 3), (col >> 4) & 3), col & 3)
-    selector = selector.T.astype(BF)
-    _, weighting = chosen_of(label_of(col >> 4, (col >> 2) & 3), col & 3)
-    WO[...] = weighting.astype(BF)
-    WT[b] = weighting.astype(BF)
+    row = lax.broadcasted_iota(jnp.int32, (128, 1), 0)
+    selector, _ = chosen_of(label_of((row >> 6) * 4 + ((row >> 2) & 3), (row >> 4) & 3), row & 3)
+    selector = selector.astype(BF)
     loads[2].wait()
 
     def pack(h, c):
@@ -99,11 +100,6 @@
             O[h, :, :, cols] = rows
             A[h, 0, :, cols] = rows[0]
 
-    for h in range(2):
-        for c in range(2):
-            pack(h, c)
-    pl.semaphore_wait(barrier, NZ * NG - 1 + NB - 1)
-
     sent = []
 
     def send(src, dst, ss, rs_, ee, bb):
@@ -123,13 +119,12 @@
     def side(c):
         return pl.ds(c * half_c, half_c)
 
-    for h in range(2):
-        for c in range(2):
-            for d in (2, 3, 1):
-                send(
-                    O.at[h, d, :, side(c)], A.at[h, d, :, side(c)],
-                    s2s.at[h, c, d], s2r.at[h, c, d], expert_at(z, d), b,
-                )
+    def quad(h, c):
+        for d in (2, 3, 1):
+            send(
+                O.at[h, d, :, side(c)], A.at[h, d, :, side(c)],
+                s2s.at[h, c, d], s2r.at[h, c, d], expert_at(z, d), b,
+            )
 
     def interleave(h, c):
         for d in (1, 2, 3):
@@ -175,6 +170,8 @@
         go(i, b, 2 + c, left + yh, c)
         if i not in XFIRST:
             go(i, b, 4 + c, me + other, c)
+        elif c == 1:
+            go(i, b, 4, me + other)
 
     def own(i):
         arrived(X.at[i, b], s3s.at[i], s3r.at[i])
@@ -216,11 +213,14 @@
             got(i, right + other, 9, 1)
             go(i, right + other, 13, left + yh, 1)
 
-    def done(i):
+    def fin(i):
         got(i, far + yh, 10, 0)
         got(i, far + yh, 11, 1)
         if i in XFIRST:
             go(i, far + yh, 7, me + other)
+
+    def done(i):
+        if i in XFIRST:
             got(i, me + other, 4)
             got(i, left + other, 5)
             got(i, right + other, 6)
@@ -369,27 +369,41 @@
         else:
             PB[...] = (pacc[...] + term).astype(BF).reshape(NB, 64, n)
 
+    pack(0, 0)
+    pl.semaphore_wait(barrier, NG - 1 + NZ - 1 + len(near))
+    quad(0, 0)
+    pack(0, 1)
+    quad(0, 1)
+    pack(1, 0)
+    pack(1, 1)
     interleave(0, 0)
     own_side(0, 0)
     interleave(0, 1)
     own_side(0, 1)
     along_z(0)
-    for j in range(1, NB):
-        send(WO, WT.at[b], ws.at[j], wr.at[j], e, peer(j))
+    quad(1, 0)
+    quad(1, 1)
+    for copy in loads[3:]:
+        copy.start()
+    _, weighting = chosen_of(label_of(row >> 4, (row >> 2) & 3), row & 3)
+    weighting = weighting.T.astype(BF)
+    WO[...] = weighting
+    WT[b] = weighting
     part(0)
+    own(1)
+    onward(0)
     interleave(1, 0)
     interleave(1, 1)
     along_z(1)
-    own(1)
-    onward(0)
     part(1)
     own(2)
-    weights()
+    own(3)
+    part(2)
     for t in range(1, 9):
+        if t + 3 < 8:
+            own(t + 3)
         if t + 2 < 8:
-            own(t + 2)
-        if t + 1 < 8:
-            part(t + 1)
+            part(t + 2)
         if t < 8:
             onward(t)
         if t == 3:
@@ -398,8 +412,16 @@
             h_part(1)
         if t == 7:
             h_part(2)
-        done(t - 1)
+        fin(t - 1)
+        if t == 8:
+            h_done(2)
+            down(2)
+        for i in range(8):
+            if t == (i + 2 if i in XFIRST else i + 1):
+                done(i)
         if t == 2:
+            for j in range(1, NB):
+                send(WO, WT.at[b], ws.at[j], wr.at[j], e, peer(j))
             gate_up(0)
             h_own(0)
         if t == 3:
@@ -409,6 +431,7 @@
             h_own(1)
             h_done(0)
             down(0)
+            weights()
         if t == 5:
             h_onward(1)
         if t == 6:
@@ -424,13 +447,12 @@
         if t == 8:
             gate_up(4)
             h_own(4)
-            h_done(2)
-            down(2)
+            combine(1)
             h_done(3)
             down(3)
             h_done(4)
             down(4)
-    for k in range(1, 5):
+    for k in range(2, 5):
         combine(k)
     for j in (4, 3, 5, 2, 6, 1, 7):
         send(PB.at[peer(j)], OB.at[b], fs.at[j], fr.at[j], e, peer(j))
@@ -457,8 +479,8 @@
         out_specs=pl.BlockSpec(memory_space=pltpu.VMEM),
         scratch_shapes=[
             pltpu.VMEM((tok, width), BF),
-            pltpu.VMEM(expert_ids.shape, jnp.int32),
-            pltpu.VMEM(gate_weights.shape, BF),
+            pltpu.VMEM(expert_ids.shape[::-1], jnp.int32),
+            pltpu.VMEM(gate_weights.shape[::-1], BF),
             pltpu.VMEM((2, NG, 16, width), BF),
             pltpu.VMEM((2, NG, 16, width), BF),
             pltpu.VMEM((units, 16, width), BF),
@@ -487,7 +509,7 @@
         compiler_params=pltpu.CompilerParams(
             collective_id=0, has_side_effects=True, vmem_limit_bytes=63 * 1024 * 1024
         ),
-    )(tokens, expert_ids, gate_weights, w_gate[0], w_up[0], w_down[0])
+    )(tokens, expert_ids.T, gate_weights.T, w_gate[0], w_up[0], w_down[0])
 
 
 def solution(mesh):

time: 217 us -> 204 us (0.940)
  Pallas kernels: 209 us -> 198 us
  local copies, waits for them, and re-layouts: 4.91 us -> 2.16 us
    pallas_call x1, Pallas kernels: 209 us -> 198 us  [on_device(): pl.pallas_call(kernel, out_shape=jax.ShapeDtypeStruct((tok, width), BF),...]
    unnamed x3 -> x1, local copies, waits for them, and re-layouts: 4.91 us -> 2.16 us
where the time goes in v4:
time: 204 us; the launch traced here: 200 us
  Pallas kernels  198 us (97%)
  local copies, waits for them, and re-layouts  2.16 us (1%)
    pallas_call x1, Pallas kernels, on_device(): pl.pallas_call(kernel, out_shape=jax.ShapeDtypeStruct((tok, width), BF),...  198 us

profile of v4, /device:TPU:56, one launch (start us, length us, event | category | flops | bytes accessed | tf_op | source)
XLA Modules:
  0.0 200.2 jit_solution(10674531187308361375)
XLA Ops:
  0.0 198.0 %shard_map.64 = bf16[64,7168]{1,0:T(8,128)(2,1)} custom-call(bf16[64,7168]{1,0:T(8,128)(2,1)} %tok_ref.1, s32[8,64]{1,0:T(8,128)} %bitcast.8, bf16[8,64]{1,0:T(8,128)(2,1)} %bitcast.9, bf16[7168,256]{1,0:T(8,128)(2,1)} %bitcast.5, bf16[7168,256]{1,0:T(8,128)(2,1)} %bitcast.6, bf16[2048,896]{1,0:T(8,128)(2,1)} %bitcast.7), custom_call_target="tpu_custom_call" | custom-call | tf_op jit(solution)/shard_map/pallas_call | solution.py:475
  198.0 2.2 %copy.8 = bf16[64,7168]{1,0:T(8,128)(2,1)} copy(bf16[64,7168]{1,0:T(8,128)(2,1)} %shard_map.64) | data formatting | bytes 1835008

commit v5 on v4

--- a/solution.py
+++ b/solution.py
@@ -13,6 +13,7 @@
 XFIRST = (2, 4)
 CHUNKS = ((0, 2), (2, 2), (4, 2), (6, 1), (7, 1))
 DIRECT = (3, 4)
+HIDDEN_XFIRST = (0, 1)
 NZ = 8
 NG = 4
 NX = 4
@@ -256,7 +257,7 @@
         h_go(k, b, 1, left + yh)
 
     def h_part(k):
-        if k in DIRECT:
+        if k in DIRECT or k in HIDDEN_XFIRST:
             return
         h_got(k, me + other, 2)
         h_go(k, me + other, 3, right + yh)
@@ -269,15 +270,31 @@
         h_go(k, left + yh, 5, right + yh, 0)
         h_got(k, right + yh, 1)
         h_go(k, right + yh, 6, left + yh, 1)
+        if k in HIDDEN_XFIRST:
+            h_go(k, left + yh, 3, me + other)
+            h_go(k, right + yh, 4, me + other)
+            return
         h_got(k, left + other, 3)
         h_go(k, left + other, 7, right + yh, 0)
         h_got(k, right + other, 4)
         h_go(k, right + other, 8, left + yh, 1)
 
+    def h_fin(k):
+        if k in HIDDEN_XFIRST:
+            h_got(k, far + yh, 5, 0)
+            h_got(k, far + yh, 6, 1)
+            h_go(k, far + yh, 7, me + other)
+
     def h_done(k):
         if k in DIRECT:
             for j in range(1, NB):
                 h_got(k, peer(j), NB - j)
+            return
+        if k in HIDDEN_XFIRST:
+            h_got(k, me + other, 2)
+            h_got(k, left + other, 3)
+            h_got(k, right + other, 4)
+            h_got(k, far + other, 7)
             return
         h_got(k, far + yh, 5, 0)
         h_got(k, far + yh, 6, 1)
@@ -414,6 +431,7 @@
             h_part(2)
         fin(t - 1)
         if t == 8:
+            h_fin(2)
             h_done(2)
             down(2)
         for i in range(8):
@@ -427,6 +445,7 @@
         if t == 3:
             h_onward(0)
         if t == 4:
+            h_fin(0)
             gate_up(1)
             h_own(1)
             h_done(0)
@@ -435,6 +454,7 @@
         if t == 5:
             h_onward(1)
         if t == 6:
+            h_fin(1)
             gate_up(2)
             h_own(2)
             h_done(1)

time: 204 us -> 200 us (0.980); the launches traced: 200 us -> 199 us
  no operation moved by 1% of the time
where the time goes in v5:
time: 200 us; the launch traced here: 199 us
  Pallas kernels  197 us (98%)
  local copies, waits for them, and re-layouts  2.16 us (1%)
    pallas_call x1, Pallas kernels, on_device(): pl.pallas_call(kernel, out_shape=jax.ShapeDtypeStruct((tok, width), BF),...  197 us

profile of v5, /device:TPU:56, one launch (start us, length us, event | category | flops | bytes accessed | tf_op | source)
XLA Modules:
  0.0 198.9 jit_solution(15082466236912883121)
XLA Ops:
  0.0 196.8 %shard_map.64 = bf16[64,7168]{1,0:T(8,128)(2,1)} custom-call(bf16[64,7168]{1,0:T(8,128)(2,1)} %tok_ref.1, s32[8,64]{1,0:T(8,128)} %bitcast.8, bf16[8,64]{1,0:T(8,128)(2,1)} %bitcast.9, bf16[7168,256]{1,0:T(8,128)(2,1)} %bitcast.5, bf16[7168,256]{1,0:T(8,128)(2,1)} %bitcast.6, bf16[2048,896]{1,0:T(8,128)(2,1)} %bitcast.7), custom_call_target="tpu_custom_call" | custom-call | tf_op jit(solution)/shard_map/pallas_call | solution.py:495
  196.8 2.2 %copy.8 = bf16[64,7168]{1,0:T(8,128)(2,1)} copy(bf16[64,7168]{1,0:T(8,128)(2,1)} %shard_map.64) | data formatting | bytes 1835008

commit v6 on v5

--- a/solution.py
+++ b/solution.py
@@ -414,13 +414,11 @@
     along_z(1)
     part(1)
     own(2)
-    own(3)
-    part(2)
     for t in range(1, 9):
-        if t + 3 < 8:
-            own(t + 3)
         if t + 2 < 8:
-            part(t + 2)
+            own(t + 2)
+        if t + 1 < 8:
+            part(t + 1)
         if t < 8:
             onward(t)
         if t == 3:

time: 200 us -> 200 us (level)
  no operation moved by 1% of the time
where the time goes in v6:
time: 200 us; the launch traced here: 199 us
  Pallas kernels  197 us (98%)
  local copies, waits for them, and re-layouts  2.16 us (1%)
    pallas_call x1, Pallas kernels, on_device(): pl.pallas_call(kernel, out_shape=jax.ShapeDtypeStruct((tok, width), BF),...  197 us

profile of v6, /device:TPU:56, one launch (start us, length us, event | category | flops | bytes accessed | tf_op | source)
XLA Modules:
  0.0 198.9 jit_solution(7034307438016677946)
XLA Ops:
  0.0 196.7 %shard_map.64 = bf16[64,7168]{1,0:T(8,128)(2,1)} custom-call(bf16[64,7168]{1,0:T(8,128)(2,1)} %tok_ref.1, s32[8,64]{1,0:T(8,128)} %bitcast.8, bf16[8,64]{1,0:T(8,128)(2,1)} %bitcast.9, bf16[7168,256]{1,0:T(8,128)(2,1)} %bitcast.5, bf16[7168,256]{1,0:T(8,128)(2,1)} %bitcast.6, bf16[2048,896]{1,0:T(8,128)(2,1)} %bitcast.7), custom_call_target="tpu_custom_call" | custom-call | tf_op jit(solution)/shard_map/pallas_call | solution.py:493
  196.7 2.2 %copy.8 = bf16[64,7168]{1,0:T(8,128)(2,1)} copy(bf16[64,7168]{1,0:T(8,128)(2,1)} %shard_map.64) | data formatting | bytes 1835008
